TPU v7x, 32 devices: a whole 2x2x4 slice. The times are simulated.
32 devices in a mesh: row: 2 (over y), col: 4 (over x, core), band: 4 (over z).
Axes of the slice: x: 2, y: 2, z: 4, core: 2. Of those that a mesh axis runs over, the one named last changes fastest.
Arguments:
- vis: bfloat16 [64, 4, 2, 512, 512], P('band', None, None, 'row', 'col'), may hold values from -200 to 200
- flags: int32 [64, 4, 512], P('band'), may hold values 0 or 1
- positions: float32 [4, 3, 512], replicated, may hold values from -4 to 4
- lmn: float32 [3, 8], replicated, may hold values from -3 to 3
- flux: float32 [64, 8], P('band'), may hold values from 0.5 to 2
- gains: float32 [64, 4, 2, 8, 512], P('band', None, None, None, ('row', 'col')), may hold values from -6 to 6
- duals: float32 [64, 4, 2, 8, 512], P('band', None, None, None, ('row', 'col')), may hold values from -2 to 2
Outputs:
- gains_out: float32 [64, 4, 2, 8, 512], P('band', None, None, None, ('row', 'col'))
- duals_out: float32 [64, 4, 2, 8, 512], P('band', None, None, None, ('row', 'col'))
All inputs are finite; a program needn't handle non-finite values. No bound on the sum of `flags` on one device may be relied on, other than what follows from the above.
Results may differ from a plain program's by a relative error of at most 0.0003.
Values sent between devices are 32-bit elements; how exact they have to be, the bound alone decides.
No kernel may reach another device: no remote copies, remote signals or barrier semaphores. Data moves between devices by JAX's collectives and lax.ppermute only.
A program may use at most 128 MiB of HBM per device.

v0:
```python
import math
import jax
import jax.numpy as jnp
from jax import lax
from jax.sharding import PartitionSpec as P

S = 512
F = 64
ITERS = 2
PENALTY = 0.05
HIGH = lax.Precision.HIGHEST


def basis(count):
    grid = 2.0 * jnp.arange(count, dtype=jnp.float32) / (count - 1) - 1.0
    return jnp.stack([grid**power for power in range(4)], axis=1)


def rotate(positions, lmn, freq):
    geometry = jnp.einsum("tks,kd->tds", positions, lmn, precision=HIGH)
    angle = 2.0 * math.pi * freq[:, None, None, None] * geometry[None]
    return (jnp.cos(angle), -jnp.sin(angle))


def complex_mul(a_re, a_im, b_re, b_im):
    return (a_re * b_re - a_im * b_im, a_re * b_im + a_im * b_re)


def solve_fit(rhs):
    full = basis(F)
    gram = jnp.dot(full.T, full, precision=HIGH)
    factor = jnp.linalg.cholesky(gram)
    flat = rhs.reshape(rhs.shape[0], -1)
    return jax.scipy.linalg.cho_solve((factor, True), flat).reshape(rhs.shape)


def shards(vis, flags, positions, lmn, flux, gains, duals):
    width = gains.shape[0]
    first = lax.axis_index("band") * width
    local_basis = lax.dynamic_slice_in_dim(basis(F), first, width, 0)
    freq = 1.0 + (first + jnp.arange(width, dtype=jnp.int32)).astype(jnp.float32) / F
    row_index = lax.axis_index("row")
    col_index = lax.axis_index("col")
    row_count = vis.shape[3]
    col_count = vis.shape[4]
    owned = gains.shape[4]
    own_start = (row_index * lax.axis_size("col") + col_index) * owned
    row_start = row_index * row_count
    col_start = col_index * col_count
    own_cos, own_sin = rotate(lax.dynamic_slice_in_dim(positions, own_start, owned, 2), lmn, freq)
    row_cos, row_sin = rotate(
        lax.dynamic_slice_in_dim(positions, row_start, row_count, 2), lmn, freq
    )
    col_cos, col_sin = rotate(
        lax.dynamic_slice_in_dim(positions, col_start, col_count, 2), lmn, freq
    )
    all_live = flags.astype(jnp.float32)
    row_live = lax.dynamic_slice_in_dim(all_live, row_start, row_count, 2)
    col_live = lax.dynamic_slice_in_dim(all_live, col_start, col_count, 2)
    own_live = lax.dynamic_slice_in_dim(all_live, own_start, owned, 2)
    row_ids = row_start + jnp.arange(row_count, dtype=jnp.int32)
    col_ids = col_start + jnp.arange(col_count, dtype=jnp.int32)
    distinct = (row_ids[:, None] != col_ids[None, :]).astype(jnp.float32)
    weight = row_live[:, :, :, None] * col_live[:, :, None, :] * distinct
    vis_re = vis[:, :, 0].astype(jnp.float32)
    vis_im = vis[:, :, 1].astype(jnp.float32)
    scale = flux[:, None, :, None]

    def fit(gain, dual):
        rhs = jnp.einsum("fk,ftcds->ktcds", local_basis, gain + dual, precision=HIGH)
        return solve_fit(lax.psum(rhs, "band"))

    gain, dual = (gains, duals)
    coeffs = fit(gain, dual)
    for step in range(ITERS):
        target = jnp.einsum("fk,ktcds->ftcds", local_basis, coeffs, precision=HIGH) - dual
        every = lax.all_gather(gain, ("row", "col"), axis=4, tiled=True)
        row_gain = lax.dynamic_slice_in_dim(every, row_start, row_count, 4)
        col_gain = lax.dynamic_slice_in_dim(every, col_start, col_count, 4)
        row_re, row_im = complex_mul(row_gain[:, :, 0], row_gain[:, :, 1], row_cos, row_sin)
        col_re, col_im = complex_mul(col_gain[:, :, 0], col_gain[:, :, 1], col_cos, col_sin)
        col_re = scale * col_re
        col_im = scale * col_im
        model_re = jnp.einsum("ftdp,ftdq->ftpq", row_re, col_re, precision=HIGH) + jnp.einsum(
            "ftdp,ftdq->ftpq", row_im, col_im, precision=HIGH
        )
        model_im = jnp.einsum("ftdp,ftdq->ftpq", row_im, col_re, precision=HIGH) - jnp.einsum(
            "ftdp,ftdq->ftpq", row_re, col_im, precision=HIGH
        )
        resid_re = weight * (vis_re - model_re)
        resid_im = weight * (vis_im - model_im)
        squares, samples = lax.psum(
            (jnp.sum(resid_re * resid_re + resid_im * resid_im), jnp.sum(weight)),
            ("row", "col", "band"),
        )
        sum_re = jnp.einsum("ftpq,ftdq->ftdp", resid_re, col_re, precision=HIGH) - jnp.einsum(
            "ftpq,ftdq->ftdp", resid_im, col_im, precision=HIGH
        )
        sum_im = jnp.einsum("ftpq,ftdq->ftdp", resid_re, col_im, precision=HIGH) + jnp.einsum(
            "ftpq,ftdq->ftdp", resid_im, col_re, precision=HIGH
        )
        pairs = lax.psum_scatter(
            jnp.stack([sum_re, sum_im], axis=2), "col", scatter_dimension=4, tiled=True
        )
        every_mag = every[:, :, 0] * every[:, :, 0] + every[:, :, 1] * every[:, :, 1]
        total_mag = jnp.einsum("ftds,fts->ftd", every_mag, all_live, precision=HIGH)
        own_mag = gain[:, :, 0] * gain[:, :, 0] + gain[:, :, 1] * gain[:, :, 1]
        own_flag = own_live[:, :, None, :]
        own_denom = (scale * scale * own_flag * (total_mag[:, :, :, None] - own_flag * own_mag))[
            :, :, None
        ]
        num_re, num_im = complex_mul(own_cos, -own_sin, pairs[:, :, 0], pairs[:, :, 1])
        numer = jnp.stack([num_re, num_im], axis=2)
        rho = PENALTY * S * (squares / samples + 1e-06)
        fresh = (numer + own_denom * gain + rho * target) / (own_denom + rho)
        gain = 0.5 * (gain + fresh)
        coeffs = fit(gain, dual)
        dual = dual + gain - jnp.einsum("fk,ktcds->ftcds", local_basis, coeffs, precision=HIGH)
    return (gain, dual)


def solution(mesh):
    return jax.shard_map(
        shards,
        mesh=mesh,
        in_specs=(
            P("band", None, None, "row", "col"),
            P("band", None, None),
            P(),
            P(),
            P("band", None),
            P("band", None, None, None, ("row", "col")),
            P("band", None, None, None, ("row", "col")),
        ),
        out_specs=(
            P("band", None, None, None, ("row", "col")),
            P("band", None, None, None, ("row", "col")),
        ),
        check_vma=False,
    )
```

profile of v0, /device:TPU:0, one launch (start us, length us, event | category | flops | bytes accessed | tf_op | source)
XLA Modules:
  0.0 711.7 jit_solution(12807473664040143431)
XLA Ops:
  8.1 3.9 copy.135
  12.0 1.3 add.237
  20.6 84.0 %all-gather.3.cloned.1.call-done = f32[16,4,2,8,512]{0,3,2,1,4:T(8,128)} async-done(((f32[16,4,2,8,64]{0,3,2,1,4:T(8,128)}), f32[16,4,2,8,512]{0,3,2,1,4:T(8,128)}) %all-gather.3.cloned.1.call-update) | async-done | bytes 2097168 | tf_op jit(solution)/shard_map/all_gather | solution.py:77
  104.6 4.0 constant_dynamic-slice_fusion.3
  108.6 2.7 copy.192
  111.3 1.3 copy.190
  112.7 7.7 %constant_dynamic-slice_fusion.2 = (f32[16,4,1,8,256]{0,3,2,1,4:T(8,128)}, f32[16,4,1,8,256]{0,3,2,1,4:T(8,128)}) fusion(f32[16,4,2,8,512]{0,3,2,1,4:T(8,128)} %all-gather.3.cloned.1.call-done, s32[]{:T(128)S(6)} %select_n.24, s32[]{:T(128)S(6)} %add.262), kind=kLoop, calls=%fused_computation.128 | loop fusion | bytes 2097160 | tf_op jit(solution)/shard_map/slice | solution.py:80
  120.4 3.8 copy.197
  124.1 3.8 copy.195
  127.9 1.4 fusion.57
  129.3 15.9 %fusion.122 = f32[16,4,256,128]{3,2,1,0:T(8,128)S(1)} fusion(f32[16,4,8,128]{3,2,1,0:T(8,128)S(1)} %get-tuple-element.34, f32[16,4,1,8,256]{4,3,1,0,2:T(8,128)S(1)} %copy.197, f32[16,4,1,8,256]{4,3,1,0,2:T(8,128)S(1)} %copy.195, f32[4,8,256]{2,1,0:T(8,128)S(1)} %convolution_bitcast_fusion, f32[16]{0:T(128)S(1)} %add_multiply_fusion), kind=kOutput, calls=%fused_computation.178 | convolution fusion | flops 201981952 | bytes 9732160 | tf_op jit(solution)/shard_map/ftdp,ftdq->ftpq/dot_general | solution.py:84
  145.2 16.0 %fusion.118 = f32[16,4,256,128]{3,2,1,0:T(8,128)S(1)} fusion(f32[16,4,8,128]{3,2,1,0:T(8,128)S(1)} %get-tuple-element.34, f32[16,4,1,8,256]{4,3,1,0,2:T(8,128)S(1)} %copy.197, f32[16,4,1,8,256]{4,3,1,0,2:T(8,128)S(1)} %copy.195, f32[4,8,256]{2,1,0:T(8,128)S(1)} %convolution_bitcast_fusion, f32[16]{0:T(128)S(1)} %add_multiply_fusion), kind=kOutput, calls=%fused_computation.177 | convolution fusion | flops 201981952 | bytes 9732160 | tf_op jit(solution)/shard_map/ftdp,ftdq->ftpq/dot_general | solution.py:87
  161.3 19.2 %fusion = f32[16,4,256,128]{3,2,1,0:T(8,128)S(1)} fusion(f32[16,4,256,128]{3,2,1,0:T(8,128)S(1)} %fusion.122, f32[256,128]{1,0:T(8,128)S(1)} %compare_convert_fusion, f32[16,4,128]{2,1,0:T(4,128)S(1)} %constant_dynamic-slice_fusion.10, f32[16,4,256]{2,1,0:T(4,128)S(1)} %constant_dynamic-slice_fusion.11, bf16[16,4,2,256,128]{4,3,2,1,0:T(8,128)(2,1)S(1)} %bitcast.197, ...), kind=kOutput, calls=%fused_computation.4 | convolution fusion | flops 214564864 | bytes 22544448 | tf_op jit(solution)/shard_map/ftdp,ftdq->ftpq/dot_general | solution.py:84
  180.5 7.2 %fusion.128 = f32[16,4,8,256]{3,2,1,0:T(8,128)S(1)} fusion(f32[16,4,8,128]{3,2,1,0:T(8,128)S(1)} %get-tuple-element.35, f32[16,4,256,128]{3,2,1,0:T(8,128)S(1)} %fusion), kind=kOutput, calls=%fused_computation.182 | convolution fusion | flops 201326592 | bytes 9175040 | tf_op jit(solution)/shard_map/ftpq,ftdq->ftdp/dot_general | solution.py:99
  187.7 7.0 fusion.127
  194.8 20.2 %add_reduce_fusion.1 = (f32[]{:T(128)}, f32[16,4,256,128]{3,2,1,0:T(8,128)S(1)}) fusion(f32[16,4,256,128]{3,2,1,0:T(8,128)S(1)} %fusion, f32[16,4,256,128]{3,2,1,0:T(8,128)S(1)} %fusion.118, f32[16,4,8,128]{3,2,1,0:T(8,128)S(1)} %get-tuple-element.35, f32[16,4,1,8,256]{4,3,1,0,2:T(8,128)S(1)} %copy.197, f32[16,4,1,8,256]{4,3,1,0,2:T(8,128)S(1)} %copy.195, ...), kind=kOutput, calls=%fused_computation.21 | convolution fusion | flops 222953472 | bytes 30933060 | tf_op jit(solution)/shard_map/ftdp,ftdq->ftpq/dot_general | solution.py:87
  215.0 7.0 fusion.14
  222.0 7.3 %fusion.13 = f32[16,4,1,8,256]{4,3,1,0,2:T(8,128)S(1)} fusion(f32[16,4,8,256]{3,2,1,0:T(8,128)S(1)} %fusion.127, f32[16,4,8,128]{3,2,1,0:T(8,128)S(1)} %get-tuple-element.35, f32[16,4,256,128]{3,2,1,0:T(8,128)S(1)} %get-tuple-element.41), kind=kOutput, calls=%fused_computation.30 | convolution fusion | flops 201457664 | bytes 9699328 | tf_op jit(solution)/shard_map/ftpq,ftdq->ftdp/dot_general | solution.py:96
  229.4 12.1 %copy.182 = f32[16,4,2,8,256]{3,1,0,2,4:T(4,128)} copy(f32[16,4,2,8,256]{4,3,1,0,2:T(8,128)S(1)} %pad_maximum_fusion) | data formatting | bytes 2097152
  241.6 22.3 %reshape.149 = f32[256,1024]{1,0:T(8,128)} reshape(f32[256,2,16,4,8]{4,3,2,1,0:T(4,128)} %bitcast.194) | data formatting | bytes 2097152
  265.4 3.1 fusion.12
  268.6 1.2 fusion.93
  270.8 40.1 %all-reduce = (f32[]{:T(128)}, f32[]{:T(128)}) all-reduce(f32[]{:T(128)} %get-tuple-element.40, f32[]{:T(128)} %fusion.12), channel_id=1, replica_groups=mesh['row'=2,'col'=4,'band'=4] {'row','col','band'}, use_global_device_ids=true, to_apply=%region_2.3 | all-reduce | flops 2 | bytes 16 | tf_op jit(solution)/shard_map/psum | solution.py:92
  312.2 7.0 fusion.11
  319.4 7.2 %reshape.150 = f32[64,2,16,4,8]{4,3,2,1,0:T(4,128)} reshape(f32[64,1024]{1,0:T(8,128)} %reduce-scatter.7.cloned.1.call-done) | data formatting | bytes 524288
  326.7 4.8 fusion.126
  331.5 2.4 copy.200
  333.8 2.4 copy.199
  336.2 1.1 fusion.52
  337.3 3.0 broadcast_multiply_fusion
  340.4 2.8 copy.155
  343.2 1.7 fusion.79
  346.3 87.7 %all-gather.5.cloned.1.call-done = f32[16,4,2,8,512]{0,3,2,1,4:T(8,128)} async-done(((f32[16,4,2,8,64]{0,3,2,1,4:T(8,128)}), f32[16,4,2,8,512]{0,3,2,1,4:T(8,128)}) %all-gather.5.cloned.1.call-update) | async-done | bytes 2097168 | tf_op jit(solution)/shard_map/all_gather | solution.py:77
  434.0 4.6 constant_dynamic-slice_fusion
  438.6 2.7 copy.203
  441.4 2.7 copy.202
  444.1 7.7 %constant_dynamic-slice_fusion.1 = (f32[16,4,1,8,256]{0,3,2,1,4:T(8,128)}, f32[16,4,1,8,256]{0,3,2,1,4:T(8,128)}) fusion(f32[16,4,2,8,512]{0,3,2,1,4:T(8,128)} %all-gather.5.cloned.1.call-done, s32[]{:T(128)S(6)} %select_n.24, s32[]{:T(128)S(6)} %add.262), kind=kLoop, calls=%fused_computation.127 | loop fusion | bytes 2097160 | tf_op jit(solution)/shard_map/slice | solution.py:80
  451.8 3.8 copy.206
  455.6 3.8 copy.205
  459.4 1.4 fusion.63
  460.8 15.9 %fusion.116 = f32[16,4,256,128]{3,2,1,0:T(8,128)S(1)} fusion(f32[16,4,8,128]{3,2,1,0:T(8,128)S(1)} %get-tuple-element.33, f32[16,4,1,8,256]{4,3,1,0,2:T(8,128)S(1)} %copy.206, f32[16,4,1,8,256]{4,3,1,0,2:T(8,128)S(1)} %copy.205, f32[4,8,256]{2,1,0:T(8,128)S(1)} %convolution_bitcast_fusion, f32[16]{0:T(128)S(1)} %add_multiply_fusion), kind=kOutput, calls=%fused_computation.176 | convolution fusion | flops 201981952 | bytes 9732160 | tf_op jit(solution)/shard_map/ftdp,ftdq->ftpq/dot_general | solution.py:84
  476.6 16.0 %fusion.112 = f32[16,4,256,128]{3,2,1,0:T(8,128)S(1)} fusion(f32[16,4,8,128]{3,2,1,0:T(8,128)S(1)} %get-tuple-element.33, f32[16,4,1,8,256]{4,3,1,0,2:T(8,128)S(1)} %copy.206, f32[16,4,1,8,256]{4,3,1,0,2:T(8,128)S(1)} %copy.205, f32[4,8,256]{2,1,0:T(8,128)S(1)} %convolution_bitcast_fusion, f32[16]{0:T(128)S(1)} %add_multiply_fusion), kind=kOutput, calls=%fused_computation.175 | convolution fusion | flops 201981952 | bytes 9732160 | tf_op jit(solution)/shard_map/ftdp,ftdq->ftpq/dot_general | solution.py:87
  492.7 19.2 %fusion.1 = f32[16,4,256,128]{3,2,1,0:T(8,128)S(1)} fusion(f32[16,4,256,128]{3,2,1,0:T(8,128)S(1)} %fusion.116, f32[256,128]{1,0:T(8,128)S(1)} %compare_convert_fusion, f32[16,4,128]{2,1,0:T(4,128)S(1)} %constant_dynamic-slice_fusion.10, f32[16,4,256]{2,1,0:T(4,128)S(1)} %constant_dynamic-slice_fusion.11, bf16[16,4,2,256,128]{4,3,2,1,0:T(8,128)(2,1)S(1)} %bitcast.199, ...), kind=kOutput, calls=%fused_computation.5 | convolution fusion | flops 214564864 | bytes 22544448 | tf_op jit(solution)/shard_map/ftdp,ftdq->ftpq/dot_general | solution.py:84
  511.9 7.2 %fusion.131 = f32[16,4,8,256]{3,2,1,0:T(8,128)S(1)} fusion(f32[16,4,8,128]{3,2,1,0:T(8,128)S(1)} %get-tuple-element.32, f32[16,4,256,128]{3,2,1,0:T(8,128)S(1)} %fusion.1), kind=kOutput, calls=%fused_computation.185 | convolution fusion | flops 201326592 | bytes 9175040 | tf_op jit(solution)/shard_map/ftpq,ftdq->ftdp/dot_general | solution.py:99
  519.2 7.0 fusion.130
  526.2 20.2 %add_reduce_fusion = (f32[]{:T(128)}, f32[16,4,256,128]{3,2,1,0:T(8,128)S(1)}) fusion(f32[16,4,256,128]{3,2,1,0:T(8,128)S(1)} %fusion.1, f32[16,4,256,128]{3,2,1,0:T(8,128)S(1)} %fusion.112, f32[16,4,8,128]{3,2,1,0:T(8,128)S(1)} %get-tuple-element.32, f32[16,4,1,8,256]{4,3,1,0,2:T(8,128)S(1)} %copy.206, f32[16,4,1,8,256]{4,3,1,0,2:T(8,128)S(1)} %copy.205, ...), kind=kOutput, calls=%fused_computation.20 | convolution fusion | flops 222953472 | bytes 30933060 | tf_op jit(solution)/shard_map/ftdp,ftdq->ftpq/dot_general | solution.py:87
  546.4 7.0 fusion.18
  553.4 7.3 %fusion.17 = f32[16,4,1,8,256]{4,3,1,0,2:T(8,128)S(1)} fusion(f32[16,4,8,256]{3,2,1,0:T(8,128)S(1)} %fusion.130, f32[16,4,8,128]{3,2,1,0:T(8,128)S(1)} %get-tuple-element.32, f32[16,4,256,128]{3,2,1,0:T(8,128)S(1)} %get-tuple-element.45), kind=kOutput, calls=%fused_computation.34 | convolution fusion | flops 201457664 | bytes 9699328 | tf_op jit(solution)/shard_map/ftpq,ftdq->ftdp/dot_general | solution.py:96
  560.8 12.1 %copy.184 = f32[16,4,2,8,256]{3,1,0,2,4:T(4,128)} copy(f32[16,4,2,8,256]{4,3,1,0,2:T(8,128)S(1)} %pad_maximum_fusion.1) | data formatting | bytes 2097152
  572.9 22.3 %reshape.151 = f32[256,1024]{1,0:T(8,128)} reshape(f32[256,2,16,4,8]{4,3,2,1,0:T(4,128)} %bitcast.195) | data formatting | bytes 2097152
  595.3 1.1 fusion.89
  596.8 39.7 %psum.48 = f32[]{:T(128)} all-reduce(f32[]{:T(128)} %get-tuple-element.44), channel_id=1, replica_groups=mesh['row'=2,'col'=4,'band'=4] {'row','col','band'}, use_global_device_ids=true, to_apply=%region_10.0 | all-reduce | flops 1 | bytes 8 | tf_op jit(solution)/shard_map/psum | solution.py:92
  637.9 7.0 fusion.7
  645.0 0.9 multiply_bitcast_fusion
  645.9 7.2 %reshape.152 = f32[64,2,16,4,8]{4,3,2,1,0:T(4,128)} reshape(f32[64,1024]{1,0:T(8,128)} %reduce-scatter.9.cloned.1.call-done) | data formatting | bytes 524288
  653.1 4.0 fusion.125
  657.1 2.4 copy.208
  659.5 1.3 copy.207
  660.8 1.1 fusion.54
  661.9 2.3 subtract_add_fusion
  665.4 1.0 copy.167
  666.4 34.3 %all-reduce.9.cloned.1.call-done = f32[4,4096]{1,0:T(4,128)} async-done(((f32[4,4096]{1,0:T(4,128)}), f32[4,4096]{1,0:T(4,128)}) %all-reduce.9.cloned.1.call-update) | async-done | bytes 65552 | tf_op jit(solution)/shard_map/psum | solution.py:71
  700.7 1.1 fusion.85
  702.9 1.0 copy.168
  (93 shorter events, 14.3 us)
Async XLA Ops:
  8.0 7.9 %copy-start = (f32[4,3,512]{2,0,1:T(4,128)S(1)}, f32[4,3,512]{2,0,1:T(4,128)}, u32[]{:S(2)}) copy-start(f32[4,3,512]{2,0,1:T(4,128)} %param.12) | copy-start | bytes 73732
  8.0 96.6 %all-gather.3.cloned.1.call-start = ((), (), s32[]{:S(2)}) async-start(), calls=%async_computation.2 | async-start | bytes 18874368 | tf_op jit(solution)/shard_map/all_gather | solution.py:77
  11.9 256.6 %all-reduce.5.cloned.1.call-start = ((), (), s32[]{:S(2)}) async-start(), calls=%async_computation.3 | async-start | bytes 131072 | tf_op jit(solution)/shard_map/psum | solution.py:71
  14.9 304.6 %reduce-scatter.7.cloned.1.call-start = ((), (), s32[]{:S(2)}) async-start(), calls=%async_computation.7 | async-start | bytes 1310720
  129.3 31.9 %slice-start = ((s8[8388608]{0:T(1024)(128)(4,1)}), s8[4194304]{0:T(1024)(128)(4,1)S(1)}, s32[]{:S(2)}) async-start(s8[8388608]{0:T(1024)(128)(4,1)} %bitcast.196), calls=%async_computation.9 | async-start | bytes 8388608
  145.2 16.1 %slice-start.1 = ((s8[8388608]{0:T(1024)(128)(4,1)}), s8[4194304]{0:T(1024)(128)(4,1)S(1)}, s32[]{:S(2)}) async-start(s8[8388608]{0:T(1024)(128)(4,1)} %bitcast.196), calls=%async_computation.10 | async-start | bytes 8388608
  241.5 22.5 %copy-start.2 = (f32[16,4,2,8,64]{4,3,2,1,0:T(8,128)S(1)}, f32[16,4,2,8,64]{4,3,2,1,0:T(8,128)}, u32[]{:S(2)}) copy-start(f32[16,4,2,8,64]{4,3,2,1,0:T(8,128)} %param.15) | copy-start | bytes 786436
  241.5 23.2 %copy-start.6 = (f32[16,8]{0,1:T(8,128)S(1)}, f32[16,8]{0,1:T(8,128)}, u32[]{:S(2)}) copy-start(f32[16,8]{0,1:T(8,128)} %param.14) | copy-start | bytes 1540
  241.5 23.7 %copy-start.7 = (f32[3,8]{1,0:T(4,128)S(1)}, f32[3,8]{1,0:T(4,128)}, u32[]{:S(2)}) copy-start(f32[3,8]{1,0:T(4,128)} %param.13) | copy-start | bytes 292
  263.9 170.1 %all-gather.5.cloned.1.call-start = ((), (), s32[]{:S(2)}) async-start(), calls=%async_computation.4 | async-start | bytes 18874368 | tf_op jit(solution)/shard_map/all_gather | solution.py:77
  319.4 18.0 %copy-start.3 = (f32[16,4,2,8,64]{4,3,2,1,0:T(8,128)S(1)}, f32[16,4,2,8,64]{4,3,2,1,0:T(8,128)}, u32[]{:S(2)}) copy-start(f32[16,4,2,8,64]{4,3,2,1,0:T(8,128)} %param.16) | copy-start | bytes 786436
  340.4 101.0 %copy-start.4 = (f32[16,4,2,8,64]{4,0,3,2,1:T(8,128)}, f32[16,4,2,8,64]{4,0,3,2,1:T(8,128)S(1)}, u32[]{:S(2)}) copy-start(f32[16,4,2,8,64]{4,0,3,2,1:T(8,128)S(1)} %get-tuple-element.42) | copy-start | bytes 786436
  343.2 252.1 %all-reduce.7.cloned.1.call-start = ((), (), s32[]{:S(2)}) async-start(), calls=%async_computation.5 | async-start | bytes 131072 | tf_op jit(solution)/shard_map/psum | solution.py:71
  345.8 300.1 %reduce-scatter.9.cloned.1.call-start = ((), (), s32[]{:S(2)}) async-start(), calls=%async_computation.8 | async-start | bytes 1310720
  460.7 31.9 %slice-start.2 = ((s8[8388608]{0:T(1024)(128)(4,1)}), s8[4194304]{0:T(1024)(128)(4,1)S(1)}, s32[]{:S(2)}) async-start(s8[8388608]{0:T(1024)(128)(4,1)} %bitcast.198), calls=%async_computation.11 | async-start | bytes 8388608
  476.6 16.1 %slice-start.3 = ((s8[8388608]{0:T(1024)(128)(4,1)}), s8[4194304]{0:T(1024)(128)(4,1)S(1)}, s32[]{:S(2)}) async-start(s8[8388608]{0:T(1024)(128)(4,1)} %bitcast.198), calls=%async_computation.12 | async-start | bytes 8388608
  595.2 105.5 %all-reduce.9.cloned.1.call-start = ((), (), s32[]{:S(2)}) async-start(), calls=%async_computation.6 | async-start | bytes 131072 | tf_op jit(solution)/shard_map/psum | solution.py:71
  637.9 7.0 copy-start.5
  653.1 50.8 %copy-start.1 = (f32[4,3,512]{2,0,1:T(4,128)S(1)}, f32[4,3,512]{2,0,1:T(4,128)}, u32[]{:S(2)}) copy-start(f32[4,3,512]{2,0,1:T(4,128)} %param.12) | copy-start | bytes 73732
Sparse Core Ops, SparseCore 0:
  12.1 92.4 all-gather.2
  264.0 24.9 reduce-scatter.6
  343.3 90.6 all-gather.4
  595.3 24.7 reduce-scatter.8
Sparse Core Ops, SparseCore 1:
  15.3 36.8 all-reduce.4
  346.0 35.0 all-reduce.6
  665.5 35.1 all-reduce.8
where the time goes:
time: 719 us; the launch traced here: 712 us
  matrix products  215 us (30%)
  waiting for transfers between devices  206 us (29%)
  local copies, waits for them, and re-layouts  163 us (23%)
  blocking collectives  79.8 us (11%)
  other arithmetic  27.9 us (4%)
  between operations  19.3 us (3%)
    all_gather x2, waiting for transfers between devices, shards(): every = lax.all_gather(gain, ('row', 'col'), axis=4, tiled=True)  172 us
    unnamed x48, local copies, waits for them, and re-layouts  124 us
    psum x2, blocking collectives, shards(): lax.psum((jnp.sum(resid_re * resid_re + resid_im * resid_im), jnp.sum(wei...  79.8 us
    dot_general x2, matrix products, shards(): jnp.einsum('ftdp,ftdq->ftpq', row_re, col_im, precision=HIGH)  40.4 us
    dot_general x2, matrix products, shards(): jnp.einsum('ftdp,ftdq->ftpq', row_im, col_im, precision=HIGH)  38.5 us
    psum x3, waiting for transfers between devices, fit(): return solve_fit(lax.psum(rhs, 'band'))  34.3 us
    dot_general x2, matrix products, shards(): jnp.einsum('ftdp,ftdq->ftpq', row_im, col_re, precision=HIGH)  32.1 us
    dot_general x2, matrix products, shards(): jnp.einsum('ftdp,ftdq->ftpq', row_re, col_re, precision=HIGH)  31.7 us
  transfers between devices with their start and end apart: 7, of which 3 were waited for; matrix products, arithmetic and copies ran while one was open for 50% of the time, Pallas kernels for 0%

commit v1 on v0

--- a/solution.py
+++ b/solution.py
@@ -9,6 +9,10 @@
 ITERS = 2
 PENALTY = 0.05
 HIGH = lax.Precision.HIGHEST
+
+
+def move_the_axis_part(xx):
+    return jnp.concatenate(lax.all_gather(xx, ("row", "col")), axis=4)
 
 
 def basis(count):
@@ -74,7 +78,7 @@
     coeffs = fit(gain, dual)
     for step in range(ITERS):
         target = jnp.einsum("fk,ktcds->ftcds", local_basis, coeffs, precision=HIGH) - dual
-        every = lax.all_gather(gain, ("row", "col"), axis=4, tiled=True)
+        every = move_the_axis_part(gain)
         row_gain = lax.dynamic_slice_in_dim(every, row_start, row_count, 4)
         col_gain = lax.dynamic_slice_in_dim(every, col_start, col_count, 4)
         row_re, row_im = complex_mul(row_gain[:, :, 0], row_gain[:, :, 1], row_cos, row_sin)

time: 719 us -> 572 us (0.80)
  waiting for transfers between devices: 206 us -> 105 us
  local copies, waits for them, and re-layouts: 163 us -> 127 us
  other arithmetic: 27.9 us -> 16.7 us
    all_gather x2, waiting for transfers between devices: 172 us -> 70.4 us  [move_the_axis_part(): return jnp.concatenate(lax.all_gather(xx, ('row', 'col')), axis=4)]
    unnamed x48 -> x52, local copies, waits for them, and re-layouts: 124 us -> 94.8 us
    slice x4 -> x0, local copies, waits for them, and re-layouts: 23.9 us -> none  [the longest x2 15.4 us: shards(): row_gain[:, :, 0]]
    reshape x0 -> x4, local copies, waits for them, and re-layouts: none -> 18.9 us  [move_the_axis_part(): return jnp.concatenate(lax.all_gather(xx, ('row', 'col')), axis=4)]
    dot_general x2 -> x0, other arithmetic: 14 us -> none  [shards(): total_mag = jnp.einsum('ftds,fts->ftd', every_mag, all_live, precision=HIGH)]
  transfers between devices with their start and end apart: 7 -> 7, of which waited for: 3 -> 3; matrix products, arithmetic and copies ran while one was open for 50% -> 56% of each run, Pallas kernels for 0% -> 0%
where the time goes in v1:
time: 572 us; the launch traced here: 567 us
  matrix products  219 us (38%)
  local copies, waits for them, and re-layouts  127 us (22%)
  waiting for transfers between devices  105 us (18%)
  blocking collectives  79.7 us (14%)
  between operations  18.7 us (3%)
  other arithmetic  16.7 us (3%)
    unnamed x52, local copies, waits for them, and re-layouts  94.8 us
    psum x2, blocking collectives, shards(): lax.psum((jnp.sum(resid_re * resid_re + resid_im * resid_im), jnp.sum(wei...  79.7 us
    all_gather x2, waiting for transfers between devices, move_the_axis_part(): return jnp.concatenate(lax.all_gather(xx, ('row', 'col')), axis=4)  70.4 us
    dot_general x2, matrix products, shards(): jnp.einsum('ftdp,ftdq->ftpq', row_re, col_im, precision=HIGH)  40.5 us
    dot_general x2, matrix products, shards(): jnp.einsum('ftdp,ftdq->ftpq', row_im, col_im, precision=HIGH)  38.9 us
    psum x3, waiting for transfers between devices, fit(): return solve_fit(lax.psum(rhs, 'band'))  34.2 us
    dot_general x2, matrix products, shards(): jnp.einsum('ftdp,ftdq->ftpq', row_im, col_re, precision=HIGH)  31.7 us
    dot_general x2, matrix products, shards(): jnp.einsum('ftdp,ftdq->ftpq', row_re, col_re, precision=HIGH)  31.7 us
  transfers between devices with their start and end apart: 7, of which 3 were waited for; matrix products, arithmetic and copies ran while one was open for 56% of the time, Pallas kernels for 0%

profile of v1, /device:TPU:0, one launch (start us, length us, event | category | flops | bytes accessed | tf_op | source)
XLA Modules:
  0.0 566.9 jit_solution(11132306234330278480)
XLA Ops:
  8.8 1.3 add.237
  10.9 0.7 reshape.149
  11.8 1.6 convert_bitcast_fusion
  13.5 0.8 copy.75
  14.3 0.9 convolution_bitcast_fusion.1
  15.2 0.9 convolution_bitcast_fusion
  16.3 33.7 %all-gather.5.cloned.1.call-done = f32[128,4,2,8,64]{4,3,2,1,0:T(8,128)} async-done(((f32[16,4,2,8,64]{4,3,2,1,0:T(8,128)}), f32[128,4,2,8,64]{4,3,2,1,0:T(8,128)}) %all-gather.5.cloned.1.call-update) | async-done | bytes 2097168 | tf_op jit(solution)/shard_map/all_gather | solution.py:15
  50.1 6.7 %copy.76 = f32[16,4,2,8,8,64]{5,4,3,1,0,2:T(8,128)} copy(f32[16,4,2,8,8,64]{5,3,2,1,0,4:T(8,128)} %bitcast.234) | data formatting | bytes 4194304 | tf_op jit(solution)/shard_map/reshape | solution.py:15
  56.7 3.4 reshape.148
  60.1 1.7 fusion.57
  61.8 15.8 %fusion.124 = f32[16,4,256,128]{3,2,1,0:T(8,128)S(1)} fusion(f32[16,4,8,128]{3,2,1,0:T(8,128)S(1)} %get-tuple-element.20, f32[16,4,2,8,512]{4,3,1,0,2:T(8,128)S(1)} %reshape.148, s32[]{:T(128)S(6)} %select_n.24, s32[]{:T(128)S(6)} %add.260, f32[4,8,256]{2,1,0:T(8,128)S(1)} %convolution_bitcast_fusion, f32[16]{0:T(128)S(1)} %add_multiply_fusion), kind=kOutput, calls=%fused_computation.179 | convolution fusion | flops 201981952 | bytes 9732616 | tf_op jit(solution)/shard_map/ftdp,ftdq->ftpq/dot_general | solution.py:88
  77.7 15.9 %fusion.120 = f32[16,4,256,128]{3,2,1,0:T(8,128)S(1)} fusion(f32[16,4,8,128]{3,2,1,0:T(8,128)S(1)} %get-tuple-element.20, f32[16,4,2,8,512]{4,3,1,0,2:T(8,128)S(1)} %reshape.148, s32[]{:T(128)S(6)} %select_n.24, s32[]{:T(128)S(6)} %add.260, f32[4,8,256]{2,1,0:T(8,128)S(1)} %convolution_bitcast_fusion, f32[16]{0:T(128)S(1)} %add_multiply_fusion), kind=kOutput, calls=%fused_computation.178 | convolution fusion | flops 201981952 | bytes 9732616 | tf_op jit(solution)/shard_map/ftdp,ftdq->ftpq/dot_general | solution.py:91
  93.6 19.5 %fusion = f32[16,4,256,128]{3,2,1,0:T(8,128)S(1)} fusion(f32[16,4,256,128]{3,2,1,0:T(8,128)S(1)} %fusion.124, f32[256,128]{1,0:T(8,128)S(1)} %compare_convert_fusion, f32[16,4,128]{2,1,0:T(4,128)S(1)} %constant_dynamic-slice_fusion.3, f32[16,4,256]{2,1,0:T(4,128)S(1)} %constant_dynamic-slice_fusion.4, bf16[16,4,2,256,128]{4,3,2,1,0:T(8,128)(2,1)S(1)} %bitcast.229, ...), kind=kOutput, calls=%fused_computation.4 | convolution fusion | flops 214564864 | bytes 22544904 | tf_op jit(solution)/shard_map/ftdp,ftdq->ftpq/dot_general | solution.py:88
  113.1 7.2 %fusion.130 = f32[16,4,8,256]{3,2,1,0:T(8,128)S(1)} fusion(f32[16,4,8,128]{3,2,1,0:T(8,128)S(1)} %get-tuple-element.21, f32[16,4,256,128]{3,2,1,0:T(8,128)S(1)} %fusion), kind=kOutput, calls=%fused_computation.183 | convolution fusion | flops 201326592 | bytes 9175040 | tf_op jit(solution)/shard_map/ftpq,ftdq->ftdp/dot_general | solution.py:103
  120.3 7.0 %fusion.129 = f32[16,4,8,256]{3,2,1,0:T(8,128)S(1)} fusion(f32[16,4,8,128]{3,2,1,0:T(8,128)S(1)} %get-tuple-element.20, f32[16,4,256,128]{3,2,1,0:T(8,128)S(1)} %fusion), kind=kOutput, calls=%fused_computation.182 | convolution fusion | flops 201326592 | bytes 9175040 | tf_op jit(solution)/shard_map/ftpq,ftdq->ftdp/dot_general | solution.py:100
  127.3 20.3 %add_reduce_fusion.1 = (f32[]{:T(128)}, f32[16,4,256,128]{3,2,1,0:T(8,128)S(1)}) fusion(f32[16,4,256,128]{3,2,1,0:T(8,128)S(1)} %fusion, f32[16,4,256,128]{3,2,1,0:T(8,128)S(1)} %fusion.120, f32[16,4,8,128]{3,2,1,0:T(8,128)S(1)} %get-tuple-element.21, f32[16,4,2,8,512]{4,3,1,0,2:T(8,128)S(1)} %reshape.148, s32[]{:T(128)S(6)} %select_n.24, s32[]{:T(128)S(6)} %add.260, ...), kind=kOutput, calls=%fused_computation.9 | convolution fusion | flops 222953472 | bytes 30933516 | tf_op jit(solution)/shard_map/ftdp,ftdq->ftpq/dot_general | solution.py:91
  147.6 7.0 %fusion.6 = f32[16,4,1,8,256]{4,3,1,0,2:T(8,128)S(1)} fusion(f32[16,4,8,256]{3,2,1,0:T(8,128)S(1)} %fusion.130, f32[16,4,8,128]{3,2,1,0:T(8,128)S(1)} %get-tuple-element.20, f32[16,4,256,128]{3,2,1,0:T(8,128)S(1)} %get-tuple-element.33), kind=kOutput, calls=%fused_computation.19 | convolution fusion | flops 201457664 | bytes 9699328 | tf_op jit(solution)/shard_map/ftpq,ftdq->ftdp/dot_general | solution.py:103
  154.6 7.2 %fusion.5 = f32[16,4,1,8,256]{4,3,1,0,2:T(8,128)S(1)} fusion(f32[16,4,8,256]{3,2,1,0:T(8,128)S(1)} %fusion.129, f32[16,4,8,128]{3,2,1,0:T(8,128)S(1)} %get-tuple-element.21, f32[16,4,256,128]{3,2,1,0:T(8,128)S(1)} %get-tuple-element.33), kind=kOutput, calls=%fused_computation.18 | convolution fusion | flops 201457664 | bytes 9699328 | tf_op jit(solution)/shard_map/ftpq,ftdq->ftdp/dot_general | solution.py:100
  161.9 12.0 %copy.110 = f32[16,4,2,8,256]{3,1,0,2,4:T(4,128)} copy(f32[16,4,2,8,256]{4,3,1,0,2:T(8,128)S(1)} %pad_maximum_fusion) | data formatting | bytes 2097152
  174.0 22.3 %reshape.166 = f32[256,1024]{1,0:T(8,128)} reshape(f32[256,2,16,4,8]{4,3,2,1,0:T(4,128)} %bitcast.226) | data formatting | bytes 2097152
  196.3 0.8 constant_dynamic-slice_fusion.1
  199.9 3.1 fusion.4
  202.9 1.1 fusion.95
  204.4 0.8 reshape.150
  205.1 40.0 %all-reduce = (f32[]{:T(128)}, f32[]{:T(128)}) all-reduce(f32[]{:T(128)} %get-tuple-element.32, f32[]{:T(128)} %fusion.4), channel_id=1, replica_groups=mesh['row'=2,'col'=4,'band'=4] {'row','col','band'}, use_global_device_ids=true, to_apply=%region_2.3 | all-reduce | flops 2 | bytes 16 | tf_op jit(solution)/shard_map/psum | solution.py:96
  245.1 3.0 fusion.19
  249.4 0.9 fusion.113
  250.4 7.2 %reshape.167 = f32[64,2,16,4,8]{4,3,2,1,0:T(4,128)} reshape(f32[64,1024]{1,0:T(8,128)} %reduce-scatter.7.cloned.1.call-done) | data formatting | bytes 524288
  257.6 4.0 fusion.128
  261.7 3.0 copy.122
  264.7 1.9 copy.121
  266.6 2.1 fusion.52
  268.7 3.2 broadcast_multiply_fusion
  273.5 36.6 %all-gather.7.cloned.1.call-done = f32[128,4,2,8,64]{4,0,3,2,1:T(8,128)} async-done(((f32[16,4,2,8,64]{4,0,3,2,1:T(8,128)}), f32[128,4,2,8,64]{4,0,3,2,1:T(8,128)}) %all-gather.7.cloned.1.call-update) | async-done | bytes 2097168 | tf_op jit(solution)/shard_map/all_gather | solution.py:15
  310.2 5.4 copy.94
  315.6 3.4 reshape.152
  319.0 1.6 fusion.63
  320.6 15.8 %fusion.118 = f32[16,4,256,128]{3,2,1,0:T(8,128)S(1)} fusion(f32[16,4,8,128]{3,2,1,0:T(8,128)S(1)} %get-tuple-element.19, f32[16,4,2,8,512]{4,3,1,0,2:T(8,128)S(1)} %reshape.152, s32[]{:T(128)S(6)} %select_n.24, s32[]{:T(128)S(6)} %add.260, f32[4,8,256]{2,1,0:T(8,128)S(1)} %convolution_bitcast_fusion, f32[16]{0:T(128)S(1)} %add_multiply_fusion), kind=kOutput, calls=%fused_computation.177 | convolution fusion | flops 201981952 | bytes 9732616 | tf_op jit(solution)/shard_map/ftdp,ftdq->ftpq/dot_general | solution.py:88
  336.5 15.9 %fusion.114 = f32[16,4,256,128]{3,2,1,0:T(8,128)S(1)} fusion(f32[16,4,8,128]{3,2,1,0:T(8,128)S(1)} %get-tuple-element.19, f32[16,4,2,8,512]{4,3,1,0,2:T(8,128)S(1)} %reshape.152, s32[]{:T(128)S(6)} %select_n.24, s32[]{:T(128)S(6)} %add.260, f32[4,8,256]{2,1,0:T(8,128)S(1)} %convolution_bitcast_fusion, f32[16]{0:T(128)S(1)} %add_multiply_fusion), kind=kOutput, calls=%fused_computation.176 | convolution fusion | flops 201981952 | bytes 9732616 | tf_op jit(solution)/shard_map/ftdp,ftdq->ftpq/dot_general | solution.py:91
  352.4 19.5 %fusion.1 = f32[16,4,256,128]{3,2,1,0:T(8,128)S(1)} fusion(f32[16,4,256,128]{3,2,1,0:T(8,128)S(1)} %fusion.118, f32[256,128]{1,0:T(8,128)S(1)} %compare_convert_fusion, f32[16,4,128]{2,1,0:T(4,128)S(1)} %constant_dynamic-slice_fusion.3, f32[16,4,256]{2,1,0:T(4,128)S(1)} %constant_dynamic-slice_fusion.4, bf16[16,4,2,256,128]{4,3,2,1,0:T(8,128)(2,1)S(1)} %bitcast.231, ...), kind=kOutput, calls=%fused_computation.5 | convolution fusion | flops 214564864 | bytes 22544904 | tf_op jit(solution)/shard_map/ftdp,ftdq->ftpq/dot_general | solution.py:88
  371.9 7.2 %fusion.133 = f32[16,4,8,256]{3,2,1,0:T(8,128)S(1)} fusion(f32[16,4,8,128]{3,2,1,0:T(8,128)S(1)} %get-tuple-element.18, f32[16,4,256,128]{3,2,1,0:T(8,128)S(1)} %fusion.1), kind=kOutput, calls=%fused_computation.186 | convolution fusion | flops 201326592 | bytes 9175040 | tf_op jit(solution)/shard_map/ftpq,ftdq->ftdp/dot_general | solution.py:103
  379.1 7.0 %fusion.132 = f32[16,4,8,256]{3,2,1,0:T(8,128)S(1)} fusion(f32[16,4,8,128]{3,2,1,0:T(8,128)S(1)} %get-tuple-element.19, f32[16,4,256,128]{3,2,1,0:T(8,128)S(1)} %fusion.1), kind=kOutput, calls=%fused_computation.185 | convolution fusion | flops 201326592 | bytes 9175040 | tf_op jit(solution)/shard_map/ftpq,ftdq->ftdp/dot_general | solution.py:100
  386.1 20.2 %add_reduce_fusion = (f32[]{:T(128)}, f32[16,4,256,128]{3,2,1,0:T(8,128)S(1)}) fusion(f32[16,4,256,128]{3,2,1,0:T(8,128)S(1)} %fusion.1, f32[16,4,256,128]{3,2,1,0:T(8,128)S(1)} %fusion.114, f32[16,4,8,128]{3,2,1,0:T(8,128)S(1)} %get-tuple-element.18, f32[16,4,2,8,512]{4,3,1,0,2:T(8,128)S(1)} %reshape.152, s32[]{:T(128)S(6)} %select_n.24, s32[]{:T(128)S(6)} %add.260, ...), kind=kOutput, calls=%fused_computation.8 | convolution fusion | flops 222953472 | bytes 30933516 | tf_op jit(solution)/shard_map/ftdp,ftdq->ftpq/dot_general | solution.py:91
  406.3 7.0 %fusion.10 = f32[16,4,1,8,256]{4,3,1,0,2:T(8,128)S(1)} fusion(f32[16,4,8,256]{3,2,1,0:T(8,128)S(1)} %fusion.133, f32[16,4,8,128]{3,2,1,0:T(8,128)S(1)} %get-tuple-element.19, f32[16,4,256,128]{3,2,1,0:T(8,128)S(1)} %get-tuple-element.37), kind=kOutput, calls=%fused_computation.23 | convolution fusion | flops 201457664 | bytes 9699328 | tf_op jit(solution)/shard_map/ftpq,ftdq->ftdp/dot_general | solution.py:103
  413.3 7.2 %fusion.9 = f32[16,4,1,8,256]{4,3,1,0,2:T(8,128)S(1)} fusion(f32[16,4,8,256]{3,2,1,0:T(8,128)S(1)} %fusion.132, f32[16,4,8,128]{3,2,1,0:T(8,128)S(1)} %get-tuple-element.18, f32[16,4,256,128]{3,2,1,0:T(8,128)S(1)} %get-tuple-element.37), kind=kOutput, calls=%fused_computation.22 | convolution fusion | flops 201457664 | bytes 9699328 | tf_op jit(solution)/shard_map/ftpq,ftdq->ftdp/dot_general | solution.py:100
  420.7 12.0 %copy.112 = f32[16,4,2,8,256]{3,1,0,2,4:T(4,128)} copy(f32[16,4,2,8,256]{4,3,1,0,2:T(8,128)S(1)} %pad_maximum_fusion.1) | data formatting | bytes 2097152
  432.7 22.3 %reshape.168 = f32[256,1024]{1,0:T(8,128)} reshape(f32[256,2,16,4,8]{4,3,2,1,0:T(4,128)} %bitcast.227) | data formatting | bytes 2097152
  455.1 1.1 fusion.91
  456.6 0.8 reshape.154
  457.3 39.7 %psum.48 = f32[]{:T(128)} all-reduce(f32[]{:T(128)} %get-tuple-element.36), channel_id=1, replica_groups=mesh['row'=2,'col'=4,'band'=4] {'row','col','band'}, use_global_device_ids=true, to_apply=%region_10.0 | all-reduce | flops 1 | bytes 8 | tf_op jit(solution)/shard_map/psum | solution.py:96
  497.0 2.1 fusion.15
  500.4 0.9 multiply_bitcast_fusion
  501.3 7.2 %reshape.169 = f32[64,2,16,4,8]{4,3,2,1,0:T(4,128)} reshape(f32[64,1024]{1,0:T(8,128)} %reduce-scatter.9.cloned.1.call-done) | data formatting | bytes 524288
  508.6 4.0 fusion.127
  512.6 2.4 copy.124
  515.0 1.3 copy.123
  516.2 1.1 fusion.54
  517.4 2.3 subtract_add_fusion
  520.1 0.7 reshape.155
  520.9 1.0 copy.104
  521.8 34.2 %all-reduce.9.cloned.1.call-done = f32[4,4096]{1,0:T(4,128)} async-done(((f32[4,4096]{1,0:T(4,128)}), f32[4,4096]{1,0:T(4,128)}) %all-reduce.9.cloned.1.call-update) | async-done | bytes 65552 | tf_op jit(solution)/shard_map/psum | solution.py:75
  556.0 1.1 fusion.87
  557.6 0.7 convolution_subtract_fusion
  558.3 1.0 copy.105
  (98 shorter events, 8.0 us)
Async XLA Ops:
  8.0 5.4 copy-start
  8.0 42.0 %all-gather.5.cloned.1.call-start = ((), (), s32[]{:S(2)}) async-start(), calls=%async_computation.5 | async-start | bytes 4718592 | tf_op jit(solution)/shard_map/all_gather | solution.py:15
  8.7 194.2 %all-reduce.5.cloned.1.call-start = ((), (), s32[]{:S(2)}) async-start(), calls=%async_computation.2 | async-start | bytes 131072 | tf_op jit(solution)/shard_map/psum | solution.py:75
  11.7 238.7 %reduce-scatter.7.cloned.1.call-start = ((), (), s32[]{:S(2)}) async-start(), calls=%async_computation.7 | async-start | bytes 1310720
  13.3 36.7 %copy-start.6 = (f32[16,4,512]{2,1,0:T(4,128)}, f32[16,4,512]{2,1,0:T(4,128)S(1)}, u32[]{:S(2)}) copy-start(f32[16,4,512]{2,1,0:T(4,128)S(1)} %get-tuple-element.31) | copy-start | bytes 393220
  15.2 62.5 %copy-start.11 = (f32[4,8,128]{2,1,0:T(8,128)}, f32[4,8,128]{2,1,0:T(8,128)S(1)}, u32[]{:S(2)}) copy-start(f32[4,8,128]{2,1,0:T(8,128)S(1)} %convolution_bitcast_fusion.1) | copy-start | bytes 49156
  61.8 31.7 %slice-start = ((s8[8388608]{0:T(1024)(128)(4,1)}), s8[4194304]{0:T(1024)(128)(4,1)S(1)}, s32[]{:S(2)}) async-start(s8[8388608]{0:T(1024)(128)(4,1)} %bitcast.228), calls=%async_computation.9 | async-start | bytes 8388608
  77.7 15.9 %slice-start.1 = ((s8[8388608]{0:T(1024)(128)(4,1)}), s8[4194304]{0:T(1024)(128)(4,1)S(1)}, s32[]{:S(2)}) async-start(s8[8388608]{0:T(1024)(128)(4,1)} %bitcast.228), calls=%async_computation.10 | async-start | bytes 8388608
  174.0 23.2 %copy-start.2 = (f32[16,4,2,8,64]{4,3,2,1,0:T(8,128)S(1)}, f32[16,4,2,8,64]{4,3,2,1,0:T(8,128)}, u32[]{:S(2)}) copy-start(f32[16,4,2,8,64]{4,3,2,1,0:T(8,128)} %param.15) | copy-start | bytes 786436
  174.0 23.6 %copy-start.13 = (f32[16,8]{0,1:T(8,128)S(1)}, f32[16,8]{0,1:T(8,128)}, u32[]{:S(2)}) copy-start(f32[16,8]{0,1:T(8,128)} %param.14) | copy-start | bytes 1540
  174.0 25.7 %copy-start.14 = (f32[3,8]{1,0:T(4,128)S(1)}, f32[3,8]{1,0:T(4,128)}, u32[]{:S(2)}) copy-start(f32[3,8]{1,0:T(4,128)} %param.13) | copy-start | bytes 292
  196.3 113.9 %all-gather.7.cloned.1.call-start = ((), (), s32[]{:S(2)}) async-start(), calls=%async_computation.6 | async-start | bytes 4718592 | tf_op jit(solution)/shard_map/all_gather | solution.py:15
  199.9 66.7 %copy-start.9 = (f32[4,8,64]{2,1,0:T(8,128)}, f32[4,8,64]{2,1,0:T(8,128)S(1)}, u32[]{:S(2)}) copy-start(f32[4,8,64]{2,1,0:T(8,128)S(1)} %convolution_bitcast_fusion.2) | copy-start | bytes 24580
  250.4 18.3 %copy-start.3 = (f32[16,4,2,8,64]{4,3,2,1,0:T(8,128)S(1)}, f32[16,4,2,8,64]{4,3,2,1,0:T(8,128)}, u32[]{:S(2)}) copy-start(f32[16,4,2,8,64]{4,3,2,1,0:T(8,128)} %param.16) | copy-start | bytes 786436
  271.9 38.2 %copy-start.7 = (f32[16,4,2,8,64]{4,0,3,2,1:T(8,128)}, f32[16,4,2,8,64]{4,0,3,2,1:T(8,128)S(1)}, u32[]{:S(2)}) copy-start(f32[16,4,2,8,64]{4,0,3,2,1:T(8,128)S(1)} %get-tuple-element.35) | copy-start | bytes 786436
  271.9 47.1 %copy-start.12 = (f32[4,8,128]{2,1,0:T(8,128)S(1)}, f32[4,8,128]{2,1,0:T(8,128)}, u32[]{:S(2)}) copy-start(f32[4,8,128]{2,1,0:T(8,128)} %copy-done.11) | copy-start | bytes 49156
  272.0 183.2 %all-reduce.7.cloned.1.call-start = ((), (), s32[]{:S(2)}) async-start(), calls=%async_computation.3 | async-start | bytes 131072 | tf_op jit(solution)/shard_map/psum | solution.py:75
  273.5 227.8 %reduce-scatter.9.cloned.1.call-start = ((), (), s32[]{:S(2)}) async-start(), calls=%async_computation.8 | async-start | bytes 1310720
  320.6 31.7 %slice-start.2 = ((s8[8388608]{0:T(1024)(128)(4,1)}), s8[4194304]{0:T(1024)(128)(4,1)S(1)}, s32[]{:S(2)}) async-start(s8[8388608]{0:T(1024)(128)(4,1)} %bitcast.230), calls=%async_computation.11 | async-start | bytes 8388608
  336.5 15.9 %slice-start.3 = ((s8[8388608]{0:T(1024)(128)(4,1)}), s8[4194304]{0:T(1024)(128)(4,1)S(1)}, s32[]{:S(2)}) async-start(s8[8388608]{0:T(1024)(128)(4,1)} %bitcast.230), calls=%async_computation.12 | async-start | bytes 8388608
  432.7 64.3 %copy-start.8 = (f32[16,4,512,1]{2,1,0,3:T(4,128)S(1)}, f32[16,4,512,1]{2,1,0,3:T(4,128)}, u32[]{:S(2)}) copy-start(f32[16,4,512,1]{2,1,0,3:T(4,128)} %get-tuple-element.30) | copy-start | bytes 393220
  432.7 67.7 %copy-start.5 = (f32[16,4,2,8,64]{4,0,3,2,1:T(8,128)S(1)}, f32[16,4,2,8,64]{4,0,3,2,1:T(8,128)}, u32[]{:S(2)}) copy-start(f32[16,4,2,8,64]{4,0,3,2,1:T(8,128)} %get-tuple-element.34) | copy-start | bytes 786436
  455.1 101.0 %all-reduce.9.cloned.1.call-start = ((), (), s32[]{:S(2)}) async-start(), calls=%async_computation.4 | async-start | bytes 131072 | tf_op jit(solution)/shard_map/psum | solution.py:75
  501.3 14.9 %copy-start.10 = (f32[4,8,64]{2,1,0:T(8,128)S(1)}, f32[4,8,64]{2,1,0:T(8,128)}, u32[]{:S(2)}) copy-start(f32[4,8,64]{2,1,0:T(8,128)} %copy-done.9) | copy-start | bytes 24580
  501.3 16.1 %copy-start.4 = (f32[16,4,2,8,64]{4,3,2,1,0:T(8,128)S(1)}, f32[16,4,2,8,64]{4,3,2,1,0:T(8,128)}, u32[]{:S(2)}) copy-start(f32[16,4,2,8,64]{4,3,2,1,0:T(8,128)} %param.16) | copy-start | bytes 786436
  508.5 50.7 %copy-start.1 = (f32[4,3,512]{2,0,1:T(4,128)S(1)}, f32[4,3,512]{2,0,1:T(4,128)}, u32[]{:S(2)}) copy-start(f32[4,3,512]{2,0,1:T(4,128)} %param.12) | copy-start | bytes 73732
Sparse Core Ops, SparseCore 0:
  10.7 39.2 all-gather.4
  196.4 24.8 reduce-scatter.6
  272.1 38.0 all-gather.6
  455.2 24.8 reduce-scatter.8
Sparse Core Ops, SparseCore 1:
  12.1 36.8 all-reduce.4
  274.8 34.7 all-reduce.6
  520.9 35.0 all-reduce.8
